TPU v7x, 32 devices: a whole 2x2x4 slice. The times are simulated.
32 devices in a mesh: sample: 8 (over z, y), space: 4 (over x, core).
Axes of the slice: x: 2, y: 2, z: 4, core: 2. Of those that a mesh axis runs over, the one named last changes fastest.
Arguments:
- features: bfloat16 [8, 64, 256, 256], P('sample', 'space'), may hold values from -6 to 6
- weight_one: bfloat16 [3, 3, 256, 256], P(None, None, None, 'sample'), may hold values from -0.125 to 0.125
- offset_one: float32 [256], replicated, may hold values from -0.5 to 0.5
- weight_two: bfloat16 [3, 3, 256, 256], P(None, None, None, 'sample'), may hold values from -0.125 to 0.125
- offset_two: float32 [256], replicated, may hold values from -0.5 to 0.5
Outputs:
- context: bfloat16 [8, 64, 256, 256], P('sample', 'space')
All inputs are finite; a program needn't handle non-finite values.
Results may differ from a plain program's by a relative error of at most 0.0047.
Values may be sent and summed in bfloat16 or wider, within the bound.
A program may use at most 192 MiB of HBM per device.

v0:
```python
import jax
import jax.numpy as jnp
from jax import lax
from jax.sharding import PartitionSpec as P

DILATION_RATE = 8


def extended(block, sides, width):
    for axis, dim in sides:
        count = lax.axis_size(axis)
        forward = [(i, i + 1) for i in range(count - 1)]
        backward = [(target, source) for source, target in forward]
        low = lax.ppermute(
            lax.slice_in_dim(block, block.shape[dim] - width, None, axis=dim), axis, forward
        )
        high = lax.ppermute(lax.slice_in_dim(block, 0, width, axis=dim), axis, backward)
        block = jnp.concatenate([low, block, high], axis=dim)
    return block


def dilated(padded_input, kernel_weights, output_rows):
    tile_width = padded_input.shape[2]
    column_count = jnp.pad(padded_input, ((0, 0), (0, 0), (DILATION_RATE, DILATION_RATE), (0, 0)))
    tap_sum = None
    for row_offset_tap in range(3):
        for column_offset_tap in range(3):
            window = column_count[
                :,
                row_offset_tap * DILATION_RATE : row_offset_tap * DILATION_RATE + output_rows,
                column_offset_tap * DILATION_RATE : column_offset_tap * DILATION_RATE + tile_width,
                :,
            ]
            product = jnp.einsum(
                "shwc,co->shwo",
                window,
                kernel_weights[row_offset_tap, column_offset_tap],
                preferred_element_type=jnp.float32,
            )
            tap_sum = product if tap_sum is None else tap_sum + product
    return tap_sum


def first_layer(padded_input, weight_one, gathered, output_rows):
    gathered = lax.all_gather(weight_one, "sample", axis=3, tiled=True)
    return dilated(padded_input, gathered, output_rows)


def second_layer(padded_input, weight_two, gathered, output_rows):
    gathered = lax.all_gather(weight_two, "sample", axis=3, tiled=True)
    return dilated(padded_input, gathered, output_rows)


def with_rim(feature_values):
    return extended(feature_values, (("space", 1),), DILATION_RATE)


def per_device(features, weight_one, offset_one, weight_two, offset_two):
    rows_dev = features.shape[1]
    kernel_one, kernel_two = (None, None)
    tap_sum = first_layer(with_rim(features), weight_one, kernel_one, rows_dev)
    hidden = jnp.maximum(tap_sum + offset_one, 0.0).astype(jnp.bfloat16)
    hidden_rows = with_rim(hidden)
    result = second_layer(hidden_rows, weight_two, kernel_two, rows_dev)
    return jnp.maximum(result + offset_two, 0.0).astype(jnp.bfloat16)


def solution(mesh):
    return jax.shard_map(
        per_device,
        mesh=mesh,
        in_specs=(
            P("sample", "space", None, None),
            P(None, None, None, "sample"),
            P(),
            P(None, None, None, "sample"),
            P(),
        ),
        out_specs=P("sample", "space", None, None),
        check_vma=False,
    )
```

profile of v0, /device:TPU:1, one launch (start us, length us, event | category | flops | bytes accessed | tf_op | source)
XLA Modules:
  0.0 146.6 jit_solution(10417974059888261316)
XLA Ops:
  6.5 0.7 all-gather.3.cloned.1.call-update
  7.3 3.1 %fusion.43 = (bf16[1,8,256,256]{3,2,1,0:T(8,128)(2,1)}, bf16[1,8,256,256]{3,2,1,0:T(8,128)(2,1)}) fusion(bf16[1,16,256,256]{3,2,1,0:T(8,128)(2,1)} %param.5), kind=kLoop, calls=%fused_computation.79 | loop fusion | bytes 4194304 | tf_op jit(solution)/shard_map/slice | solution.py:15
  10.4 4.5 %collective-permute-start = (bf16[1,8,256,256]{3,2,1,0:T(8,128)(2,1)}, bf16[1,8,256,256]{3,2,1,0:T(8,128)(2,1)S(1)}, u32[]{:S(2)}, u32[]{:S(2)}) collective-permute-start(bf16[1,8,256,256]{3,2,1,0:T(8,128)(2,1)} %get-tuple-element.7), channel_id=1, source_target_pairs={{0,1},{1,2},{2,3},{4,5},{5,6},{6,7},{8,9},{9,10},{10,11},{12,13},{... | collective-permute-start | bytes 3145736 | tf_op jit(solution)/shard_map/ppermute | solution.py:14
  14.9 1.9 %collective-permute-start.1 = (bf16[1,8,256,256]{3,2,1,0:T(8,128)(2,1)}, bf16[1,8,256,256]{3,2,1,0:T(8,128)(2,1)}, u32[]{:S(2)}, u32[]{:S(2)}) collective-permute-start(bf16[1,8,256,256]{3,2,1,0:T(8,128)(2,1)} %get-tuple-element.8), channel_id=1, source_target_pairs={{1,0},{2,1},{3,2},{5,4},{6,5},{7,6},{9,8},{10,9},{11,10},{13,12},{... | collective-permute-start | bytes 3145736 | tf_op jit(solution)/shard_map/ppermute | solution.py:17
  16.8 10.1 %collective-permute-done = bf16[1,8,256,256]{3,2,1,0:T(8,128)(2,1)S(1)} collective-permute-done((bf16[1,8,256,256]{3,2,1,0:T(8,128)(2,1)}, bf16[1,8,256,256]{3,2,1,0:T(8,128)(2,1)S(1)}, u32[]{:S(2)}, u32[]{:S(2)}) %collective-permute-start) | collective-permute-done | bytes 1048608 | tf_op jit(solution)/shard_map/ppermute | solution.py:14
  26.9 4.7 %collective-permute-done.1 = bf16[1,8,256,256]{3,2,1,0:T(8,128)(2,1)} collective-permute-done((bf16[1,8,256,256]{3,2,1,0:T(8,128)(2,1)}, bf16[1,8,256,256]{3,2,1,0:T(8,128)(2,1)}, u32[]{:S(2)}, u32[]{:S(2)}) %collective-permute-start.1) | collective-permute-done | bytes 1048608 | tf_op jit(solution)/shard_map/ppermute | solution.py:17
  31.6 3.5 %fusion.5 = bf16[1,32,272,256]{3,2,1,0:T(8,128)(2,1)} fusion(bf16[1,8,256,256]{3,2,1,0:T(8,128)(2,1)} %collective-permute-done.1, bf16[1,16,256,256]{3,2,1,0:T(8,128)(2,1)S(1)} %copy-done.1, bf16[1,8,256,256]{3,2,1,0:T(8,128)(2,1)S(1)} %collective-permute-done), kind=kLoop, calls=%fused_computation.9 | loop fusion | flops 26738688 | bytes 8650752 | tf_op jit(solution)/shard_map/concatenate | solution.py:18
  35.1 16.4 %all-gather.3.cloned.1.call-done = bf16[3,3,256,256]{2,3,1,0:T(8,128)(2,1)} async-done(((bf16[3,3,256,32]{2,3,1,0:T(8,128)(2,1)}), bf16[3,3,256,256]{2,3,1,0:T(8,128)(2,1)}) %all-gather.3.cloned.1.call-update) | async-done | bytes 1179664 | tf_op jit(solution)/shard_map/all_gather | solution.py:45
  51.5 4.5 %fusion.25 = f32[16,256,256]{2,1,0:T(8,128)} fusion(bf16[1,32,272,256]{3,2,1,0:T(8,128)(2,1)} %fusion.5, bf16[3,3,256,256]{2,3,1,0:T(8,128)(2,1)} %all-gather.3.cloned.1.call-done), kind=kOutput, calls=%fused_computation.39 | convolution fusion | flops 536870912 | bytes 6422528 | tf_op jit(solution)/shard_map/shwc,co->shwo/dot_general | solution.py:34
  56.1 2.7 %fusion.26 = f32[16,256,256]{2,1,0:T(8,128)} fusion(bf16[1,32,272,256]{3,2,1,0:T(8,128)(2,1)S(1)} %copy-done, bf16[3,3,256,256]{2,3,1,0:T(8,128)(2,1)S(1)} %copy-done.6), kind=kOutput, calls=%fused_computation.41 | convolution fusion | flops 536870912 | bytes 6422528 | tf_op jit(solution)/shard_map/shwc,co->shwo/dot_general | solution.py:34
  58.8 2.7 %fusion.27 = f32[16,256,256]{2,1,0:T(8,128)} fusion(bf16[1,32,272,256]{3,2,1,0:T(8,128)(2,1)S(1)} %copy-done, bf16[3,3,256,256]{2,3,1,0:T(8,128)(2,1)S(1)} %copy-done.6), kind=kOutput, calls=%fused_computation.43 | convolution fusion | flops 536870912 | bytes 6422528 | tf_op jit(solution)/shard_map/shwc,co->shwo/dot_general | solution.py:34
  61.5 2.7 %fusion.28 = f32[16,256,256]{2,1,0:T(8,128)} fusion(bf16[1,32,272,256]{3,2,1,0:T(8,128)(2,1)S(1)} %copy-done, bf16[3,3,256,256]{2,3,1,0:T(8,128)(2,1)S(1)} %copy-done.6), kind=kOutput, calls=%fused_computation.45 | convolution fusion | flops 536870912 | bytes 6422528 | tf_op jit(solution)/shard_map/shwc,co->shwo/dot_general | solution.py:34
  64.2 2.7 %fusion.33 = f32[16,256,256]{2,1,0:T(8,128)} fusion(bf16[1,32,272,256]{3,2,1,0:T(8,128)(2,1)S(1)} %copy-done, bf16[3,3,256,256]{2,3,1,0:T(8,128)(2,1)S(1)} %copy-done.6), kind=kOutput, calls=%fused_computation.51 | convolution fusion | flops 536870912 | bytes 6422528 | tf_op jit(solution)/shard_map/shwc,co->shwo/dot_general | solution.py:34
  66.9 2.1 %fusion.22 = f32[16,256,256]{2,1,0:T(8,128)S(1)} fusion(bf16[1,8,256,256]{3,2,1,0:T(8,128)(2,1)} %collective-permute-done.1, bf16[1,16,256,256]{3,2,1,0:T(8,128)(2,1)S(1)} %copy-done.1, bf16[3,3,256,256]{2,3,1,0:T(8,128)(2,1)S(1)} %copy-done.6), kind=kOutput, calls=%fused_computation.36 | convolution fusion | flops 537919488 | bytes 7471104 | tf_op jit(solution)/shard_map/shwc,co->shwo/dot_general | solution.py:34
  68.9 2.7 %fusion.30 = f32[16,256,256]{2,1,0:T(8,128)} fusion(bf16[1,16,256,256]{3,2,1,0:T(8,128)(2,1)S(1)} %copy-done.1, bf16[1,8,256,256]{3,2,1,0:T(8,128)(2,1)S(1)} %copy-done.3, bf16[3,3,256,256]{2,3,1,0:T(8,128)(2,1)S(1)} %copy-done.6), kind=kOutput, calls=%fused_computation.48 | convolution fusion | flops 537919488 | bytes 7471104 | tf_op jit(solution)/shard_map/shwc,co->shwo/dot_general | solution.py:34
  71.7 2.8 %fusion.34 = f32[16,256,256]{2,1,0:T(8,128)} fusion(bf16[1,16,256,256]{3,2,1,0:T(8,128)(2,1)S(1)} %copy-done.1, bf16[3,3,256,256]{2,3,1,0:T(8,128)(2,1)S(1)} %copy-done.6), kind=kOutput, calls=%fused_computation.52 | convolution fusion | flops 536870912 | bytes 6422528 | tf_op jit(solution)/shard_map/shwc,co->shwo/dot_general | solution.py:34
  74.5 10.8 %maximum_convert_fusion.1 = bf16[16,256,256]{2,1,0:T(8,128)(2,1)S(1)} fusion(f32[16,256,256]{2,1,0:T(8,128)S(1)} %fusion.22, f32[16,256,256]{2,1,0:T(8,128)} %fusion.25, f32[16,256,256]{2,1,0:T(8,128)} %fusion.26, f32[16,256,256]{2,1,0:T(8,128)} %fusion.34, f32[16,256,256]{2,1,0:T(8,128)} %fusion.27, f32[16,256,256]{2,1,0:T(8,128)} %fusion.28, ...), kind=kOutput, calls=%fused_computation.11 | convolution fusion | flops 548405248 | bytes 37880832 | tf_op jit(solution)/shard_map/shwc,co->shwo/dot_general | solution.py:34
  85.3 1.5 %fusion.42 = (bf16[1,8,256,256]{3,2,1,0:T(8,128)(2,1)}, bf16[1,8,256,256]{3,2,1,0:T(8,128)(2,1)}) fusion(bf16[1,16,256,256]{3,2,1,0:T(8,128)(2,1)S(1)} %bitcast.169), kind=kLoop, calls=%fused_computation.78 | loop fusion | bytes 4194304 | tf_op jit(solution)/shard_map/slice | solution.py:15
  86.8 4.9 %collective-permute-start.2 = (bf16[1,8,256,256]{3,2,1,0:T(8,128)(2,1)}, bf16[1,8,256,256]{3,2,1,0:T(8,128)(2,1)S(1)}, u32[]{:S(2)}, u32[]{:S(2)}) collective-permute-start(bf16[1,8,256,256]{3,2,1,0:T(8,128)(2,1)} %get-tuple-element.5), channel_id=1, source_target_pairs={{0,1},{1,2},{2,3},{4,5},{5,6},{6,7},{8,9},{9,10},{10,11},{12,13},{... | collective-permute-start | bytes 3145736 | tf_op jit(solution)/shard_map/ppermute | solution.py:14
  91.7 2.1 %collective-permute-start.3 = (bf16[1,8,256,256]{3,2,1,0:T(8,128)(2,1)}, bf16[1,8,256,256]{3,2,1,0:T(8,128)(2,1)}, u32[]{:S(2)}, u32[]{:S(2)}) collective-permute-start(bf16[1,8,256,256]{3,2,1,0:T(8,128)(2,1)} %get-tuple-element.6), channel_id=1, source_target_pairs={{1,0},{2,1},{3,2},{5,4},{6,5},{7,6},{9,8},{10,9},{11,10},{13,12},{... | collective-permute-start | bytes 3145736 | tf_op jit(solution)/shard_map/ppermute | solution.py:17
  93.8 3.7 %fusion.37 = f32[16,256,256]{2,1,0:T(8,128)} fusion(bf16[16,256,256]{2,1,0:T(8,128)(2,1)S(1)} %maximum_convert_fusion.1, bf16[3,3,256,256]{2,3,1,0:T(8,128)(2,1)} %all-gather.5.cloned.1.call-done), kind=kOutput, calls=%fused_computation.60 | convolution fusion | flops 536870912 | bytes 6422528 | tf_op jit(solution)/shard_map/shwc,co->shwo/dot_general | solution.py:34
  97.5 6.2 %collective-permute-done.2 = bf16[1,8,256,256]{3,2,1,0:T(8,128)(2,1)S(1)} collective-permute-done((bf16[1,8,256,256]{3,2,1,0:T(8,128)(2,1)}, bf16[1,8,256,256]{3,2,1,0:T(8,128)(2,1)S(1)}, u32[]{:S(2)}, u32[]{:S(2)}) %collective-permute-start.2) | collective-permute-done | bytes 1048608 | tf_op jit(solution)/shard_map/ppermute | solution.py:14
  103.7 0.7 fusion.16
  104.7 3.4 %collective-permute-done.3 = bf16[1,8,256,256]{3,2,1,0:T(8,128)(2,1)} collective-permute-done((bf16[1,8,256,256]{3,2,1,0:T(8,128)(2,1)}, bf16[1,8,256,256]{3,2,1,0:T(8,128)(2,1)}, u32[]{:S(2)}, u32[]{:S(2)}) %collective-permute-start.3) | collective-permute-done | bytes 1048608 | tf_op jit(solution)/shard_map/ppermute | solution.py:17
  108.1 2.1 %select_maximum_fusion = bf16[1,32,272,256]{3,2,1,0:T(8,128)(2,1)S(1)} fusion(bf16[1,8,256,256]{3,2,1,0:T(8,128)(2,1)} %collective-permute-done.3, bf16[1,16,256,256]{3,2,1,0:T(8,128)(2,1)S(1)} %bitcast.171, bf16[1,8,256,256]{3,2,1,0:T(8,128)(2,1)} %copy-done.4), kind=kLoop, calls=%fused_computation.3 | loop fusion | flops 26738688 | bytes 8650752 | tf_op jit(solution)/shard_map/concatenate | solution.py:18
  110.2 2.7 %fusion.11 = f32[16,256,256]{2,1,0:T(8,128)} fusion(bf16[1,32,272,256]{3,2,1,0:T(8,128)(2,1)S(1)} %select_maximum_fusion, bf16[3,3,256,256]{2,3,1,0:T(8,128)(2,1)S(1)} %copy-done.5), kind=kOutput, calls=%fused_computation.19 | convolution fusion | flops 536870912 | bytes 6422528 | tf_op jit(solution)/shard_map/shwc,co->shwo/dot_general | solution.py:34
  112.9 2.7 %fusion.12 = f32[16,256,256]{2,1,0:T(8,128)} fusion(bf16[1,32,272,256]{3,2,1,0:T(8,128)(2,1)S(1)} %select_maximum_fusion, bf16[3,3,256,256]{2,3,1,0:T(8,128)(2,1)S(1)} %copy-done.5), kind=kOutput, calls=%fused_computation.21 | convolution fusion | flops 536870912 | bytes 6422528 | tf_op jit(solution)/shard_map/shwc,co->shwo/dot_general | solution.py:34
  115.6 2.7 %fusion.13 = f32[16,256,256]{2,1,0:T(8,128)} fusion(bf16[1,32,272,256]{3,2,1,0:T(8,128)(2,1)S(1)} %select_maximum_fusion, bf16[3,3,256,256]{2,3,1,0:T(8,128)(2,1)S(1)} %copy-done.5), kind=kOutput, calls=%fused_computation.23 | convolution fusion | flops 536870912 | bytes 6422528 | tf_op jit(solution)/shard_map/shwc,co->shwo/dot_general | solution.py:34
  118.3 2.7 %fusion.14 = f32[16,256,256]{2,1,0:T(8,128)} fusion(bf16[1,32,272,256]{3,2,1,0:T(8,128)(2,1)S(1)} %select_maximum_fusion, bf16[3,3,256,256]{2,3,1,0:T(8,128)(2,1)S(1)} %copy-done.5), kind=kOutput, calls=%fused_computation.25 | convolution fusion | flops 536870912 | bytes 6422528 | tf_op jit(solution)/shard_map/shwc,co->shwo/dot_general | solution.py:34
  121.0 2.7 %fusion.19 = f32[16,256,256]{2,1,0:T(8,128)} fusion(bf16[1,32,272,256]{3,2,1,0:T(8,128)(2,1)S(1)} %select_maximum_fusion, bf16[3,3,256,256]{2,3,1,0:T(8,128)(2,1)S(1)} %copy-done.5), kind=kOutput, calls=%fused_computation.31 | convolution fusion | flops 536870912 | bytes 6422528 | tf_op jit(solution)/shard_map/shwc,co->shwo/dot_general | solution.py:34
  123.7 4.0 %fusion.8 = f32[16,256,256]{2,1,0:T(8,128)} fusion(bf16[1,8,256,256]{3,2,1,0:T(8,128)(2,1)} %collective-permute-done.3, bf16[1,16,256,256]{3,2,1,0:T(8,128)(2,1)S(1)} %bitcast.172, bf16[3,3,256,256]{2,3,1,0:T(8,128)(2,1)S(1)} %copy-done.5), kind=kOutput, calls=%fused_computation.16 | convolution fusion | flops 537919488 | bytes 7471104 | tf_op jit(solution)/shard_map/shwc,co->shwo/dot_general | solution.py:34
  127.7 12.1 %fusion.36 = bf16[1,16,256,256]{3,2,1,0:T(8,128)(2,1)} fusion(f32[256]{0:T(256)S(1)} %copy-done.8, bf16[1,32,272,256]{3,2,1,0:T(8,128)(2,1)S(1)} %select_maximum_fusion, f32[16,256,256]{2,1,0:T(8,128)} %fusion.8, f32[16,256,256]{2,1,0:T(8,128)} %fusion.11, f32[16,256,256]{2,1,0:T(8,128)} %fusion.12, f32[16,256,256]{2,1,0:T(8,128)} %fusion.37, ...), kind=kOutput, calls=%fused_computation.54 | convolution fusion | flops 548405248 | bytes 37880832 | tf_op jit(solution)/shard_map/shwc,co->shwo/dot_general | solution.py:34
  (22 shorter events, 0.3 us)
Async XLA Ops:
  6.5 25.1 %copy-start.1 = (bf16[1,16,256,256]{3,2,1,0:T(8,128)(2,1)S(1)}, bf16[1,16,256,256]{3,2,1,0:T(8,128)(2,1)}, u32[]{:S(2)}) copy-start(bf16[1,16,256,256]{3,2,1,0:T(8,128)(2,1)} %param.5) | copy-start | bytes 6291460
  6.5 45.0 %all-gather.3.cloned.1.call-start = ((), (), s32[]{:S(2)}) async-start(), calls=%async_computation | async-start | bytes 1327104 | tf_op jit(solution)/shard_map/all_gather | solution.py:45
  7.3 86.6 %all-gather.5.cloned.1.call-start = ((), (), s32[]{:S(2)}) async-start(), calls=%async_computation.1 | async-start | bytes 1327104 | tf_op jit(solution)/shard_map/all_gather | solution.py:50
  10.4 16.5 %collective-permute-start = (bf16[1,8,256,256]{3,2,1,0:T(8,128)(2,1)}, bf16[1,8,256,256]{3,2,1,0:T(8,128)(2,1)S(1)}, u32[]{:S(2)}, u32[]{:S(2)}) collective-permute-start(bf16[1,8,256,256]{3,2,1,0:T(8,128)(2,1)} %get-tuple-element.7), channel_id=1, source_target_pairs={{0,1},{1,2},{2,3},{4,5},{5,6},{6,7},{8,9},{9,10},{10,11},{12,13},{... | collective-permute-start | bytes 3145736 | tf_op jit(solution)/shard_map/ppermute | solution.py:14
  14.9 16.7 %collective-permute-start.1 = (bf16[1,8,256,256]{3,2,1,0:T(8,128)(2,1)}, bf16[1,8,256,256]{3,2,1,0:T(8,128)(2,1)}, u32[]{:S(2)}, u32[]{:S(2)}) collective-permute-start(bf16[1,8,256,256]{3,2,1,0:T(8,128)(2,1)} %get-tuple-element.8), channel_id=1, source_target_pairs={{1,0},{2,1},{3,2},{5,4},{6,5},{7,6},{9,8},{10,9},{11,10},{13,12},{... | collective-permute-start | bytes 3145736 | tf_op jit(solution)/shard_map/ppermute | solution.py:17
  26.9 8.2 %copy-start.2 = (bf16[1,8,256,256]{3,2,1,0:T(8,128)(2,1)}, bf16[1,8,256,256]{3,2,1,0:T(8,128)(2,1)S(1)}, u32[]{:S(2)}) copy-start(bf16[1,8,256,256]{3,2,1,0:T(8,128)(2,1)S(1)} %collective-permute-done) | copy-start | bytes 3145732
  51.5 4.5 %copy-start = (bf16[1,32,272,256]{3,2,1,0:T(8,128)(2,1)S(1)}, bf16[1,32,272,256]{3,2,1,0:T(8,128)(2,1)}, u32[]{:S(2)}) copy-start(bf16[1,32,272,256]{3,2,1,0:T(8,128)(2,1)} %fusion.5) | copy-start | bytes 13369348
  51.5 4.5 %copy-start.6 = (bf16[3,3,256,256]{2,3,1,0:T(8,128)(2,1)S(1)}, bf16[3,3,256,256]{2,3,1,0:T(8,128)(2,1)}, u32[]{:S(2)}) copy-start(bf16[3,3,256,256]{2,3,1,0:T(8,128)(2,1)} %all-gather.3.cloned.1.call-done) | copy-start | bytes 3538948
  66.9 2.1 %copy-start.3 = (bf16[1,8,256,256]{3,2,1,0:T(8,128)(2,1)S(1)}, bf16[1,8,256,256]{3,2,1,0:T(8,128)(2,1)}, u32[]{:S(2)}) copy-start(bf16[1,8,256,256]{3,2,1,0:T(8,128)(2,1)} %copy-done.2) | copy-start | bytes 3145732
  71.7 2.8 %copy-start.7 = (f32[256]{0:T(256)S(1)}, f32[256]{0:T(256)}, u32[]{:S(2)}) copy-start(f32[256]{0:T(256)} %param.7) | copy-start | bytes 3076
  86.8 16.9 %collective-permute-start.2 = (bf16[1,8,256,256]{3,2,1,0:T(8,128)(2,1)}, bf16[1,8,256,256]{3,2,1,0:T(8,128)(2,1)S(1)}, u32[]{:S(2)}, u32[]{:S(2)}) collective-permute-start(bf16[1,8,256,256]{3,2,1,0:T(8,128)(2,1)} %get-tuple-element.5), channel_id=1, source_target_pairs={{0,1},{1,2},{2,3},{4,5},{5,6},{6,7},{8,9},{9,10},{10,11},{12,13},{... | collective-permute-start | bytes 3145736 | tf_op jit(solution)/shard_map/ppermute | solution.py:14
  91.7 16.4 %collective-permute-start.3 = (bf16[1,8,256,256]{3,2,1,0:T(8,128)(2,1)}, bf16[1,8,256,256]{3,2,1,0:T(8,128)(2,1)}, u32[]{:S(2)}, u32[]{:S(2)}) collective-permute-start(bf16[1,8,256,256]{3,2,1,0:T(8,128)(2,1)} %get-tuple-element.6), channel_id=1, source_target_pairs={{1,0},{2,1},{3,2},{5,4},{6,5},{7,6},{9,8},{10,9},{11,10},{13,12},{... | collective-permute-start | bytes 3145736 | tf_op jit(solution)/shard_map/ppermute | solution.py:17
  93.8 9.9 %copy-start.5 = (bf16[3,3,256,256]{2,3,1,0:T(8,128)(2,1)S(1)}, bf16[3,3,256,256]{2,3,1,0:T(8,128)(2,1)}, u32[]{:S(2)}) copy-start(bf16[3,3,256,256]{2,3,1,0:T(8,128)(2,1)} %all-gather.5.cloned.1.call-done) | copy-start | bytes 3538948
  103.7 1.0 copy-start.4
  123.7 4.0 %copy-start.8 = (f32[256]{0:T(256)S(1)}, f32[256]{0:T(256)}, u32[]{:S(2)}) copy-start(f32[256]{0:T(256)} %param.9) | copy-start | bytes 3076
Sparse Core Ops, SparseCore 0:
  9.5 41.9 all-gather.2
  53.7 39.8 all-gather.4
where the time goes:
time: 147 us
  matrix products  67.7 us (46%)
  waiting for transfers between devices  41.6 us (28%)
  starting transfers between devices  13.5 us (9%)
  between operations  13.5 us (9%)
  other arithmetic  5.53 us (4%)
  local copies, waits for them, and re-layouts  4.85 us (3%)
    dot_general x18, matrix products, dilated(): jnp.einsum('shwc,co->shwo', window, kernel_weights[row_offset_tap, column...  67.7 us
    all_gather x1, waiting for transfers between devices, first_layer(): gathered = lax.all_gather(weight_one, 'sample', axis=3, tiled=True)  16.4 us
    ppermute x2, waiting for transfers between devices, extended(): lax.ppermute(lax.slice_in_dim(block, block.shape[dim] - width, None, axis...  16.3 us
    ppermute x2, starting transfers between devices, extended(): lax.ppermute(lax.slice_in_dim(block, block.shape[dim] - width, None, axis...  9.39 us
    ppermute x2, waiting for transfers between devices, extended(): lax.ppermute(lax.slice_in_dim(block, 0, width, axis=dim), axis, backward)  8.11 us
    concatenate x2, other arithmetic, extended(): block = jnp.concatenate([low, block, high], axis=dim)  5.53 us
    slice x2, local copies, waits for them, and re-layouts, extended(): lax.slice_in_dim(block, block.shape[dim] - width, None, axis=dim)  4.59 us
    ppermute x2, starting transfers between devices, extended(): lax.ppermute(lax.slice_in_dim(block, 0, width, axis=dim), axis, backward)  4.02 us
  transfers between devices with their start and end apart: 6, of which 5 were waited for; matrix products, arithmetic and copies ran while one was open for 31% of the time, Pallas kernels for 0%

commit v1 on v0

--- a/solution.py
+++ b/solution.py
@@ -4,6 +4,12 @@
 from jax.sharding import PartitionSpec as P
 
 DILATION_RATE = 8
+
+
+def joined_along(blocks, dim):
+    blocks = jnp.moveaxis(blocks, 0, dim)
+    shape = blocks.shape
+    return blocks.reshape(*shape[:dim], shape[dim] * shape[dim + 1], *shape[dim + 2 :])
 
 
 def extended(block, sides, width):
@@ -42,7 +48,19 @@
 
 
 def first_layer(padded_input, weight_one, gathered, output_rows):
-    gathered = lax.all_gather(weight_one, "sample", axis=3, tiled=True)
+    size = lax.axis_size("sample")
+    pairs = [(i_2, (i_2 + 1) % size) for i_2 in range(size)]
+    back = [(b, a) for a, b in pairs]
+    lower, upper = ([], [])
+    for step in range(size - 1):
+        if step % 2 == 0:
+            lower.append(lax.ppermute(lower[-1] if lower else weight_one, "sample", pairs))
+        else:
+            upper.append(lax.ppermute(upper[-1] if upper else weight_one, "sample", back))
+    blocks = jnp.stack([*lower[::-1], weight_one, *upper])
+    shift = lax.axis_index("sample") - len(lower)
+    blocks = blocks[(jnp.arange(size) - shift) % size]
+    gathered = joined_along(blocks, 3)
     return dilated(padded_input, gathered, output_rows)
 
 

time: 147 us -> 152 us (1.034)
  waiting for transfers between devices: 41.6 us -> 20.8 us
  starting transfers between devices: 13.5 us -> 29 us
  local copies, waits for them, and re-layouts: 4.85 us -> 12.7 us
  matrix products: 67.7 us -> 71.8 us
    all_gather x1 -> x0, waiting for transfers between devices: 16.4 us -> none  [first_layer(): gathered = lax.all_gather(weight_one, 'sample', axis=3, tiled=True)]
    ppermute x0 -> x7, starting transfers between devices: none -> 15 us  [the longest x3 12.9 us: first_layer(): lax.ppermute(upper[-1] if upper else weight_one, 'sample', back)]
    ppermute x0 -> x7, waiting for transfers between devices: none -> 12.8 us  [the longest x4 9.8 us: first_layer(): lax.ppermute(lower[-1] if lower else weight_one, 'sample', pairs)]
    ppermute x2, waiting for transfers between devices: 16.3 us -> 6.21 us  [extended(): lax.ppermute(lax.slice_in_dim(block, block.shape[dim] - width, None, axis...]
    ppermute x2, waiting for transfers between devices: 8.11 us -> 1.72 us  [extended(): lax.ppermute(lax.slice_in_dim(block, 0, width, axis=dim), axis, backward)]
    unnamed x18 -> x19, local copies, waits for them, and re-layouts: 0.26 us -> 5.36 us
    dot_general x18, matrix products: 67.7 us -> 71.8 us  [dilated(): jnp.einsum('shwc,co->shwo', window, kernel_weights[row_offset_tap, column...]
    gather x0 -> x1, local copies, waits for them, and re-layouts: none -> 2.04 us  [first_layer(): blocks = blocks[(jnp.arange(size) - shift) % size]]
  transfers between devices with their start and end apart: 6 -> 12, of which waited for: 5 -> 7; matrix products, arithmetic and copies ran while one was open for 31% -> 37% of each run, Pallas kernels for 0% -> 0%
where the time goes in v1:
time: 152 us
  matrix products  71.8 us (47%)
  starting transfers between devices  29 us (19%)
  waiting for transfers between devices  20.8 us (14%)
  between operations  13.5 us (9%)
  local copies, waits for them, and re-layouts  12.7 us (8%)
  other arithmetic  4.05 us (3%)
    dot_general x18, matrix products, dilated(): jnp.einsum('shwc,co->shwo', window, kernel_weights[row_offset_tap, column...  71.8 us
    ppermute x3, starting transfers between devices, first_layer(): lax.ppermute(upper[-1] if upper else weight_one, 'sample', back)  12.9 us
    ppermute x2, starting transfers between devices, extended(): lax.ppermute(lax.slice_in_dim(block, block.shape[dim] - width, None, axis...  9.98 us
    ppermute x4, waiting for transfers between devices, first_layer(): lax.ppermute(lower[-1] if lower else weight_one, 'sample', pairs)  9.8 us
    ppermute x2, waiting for transfers between devices, extended(): lax.ppermute(lax.slice_in_dim(block, block.shape[dim] - width, None, axis...  6.21 us
    unnamed x19, local copies, waits for them, and re-layouts  5.36 us
    slice x2, local copies, waits for them, and re-layouts, extended(): lax.slice_in_dim(block, block.shape[dim] - width, None, axis=dim)  4.49 us
    concatenate x2, other arithmetic, extended(): block = jnp.concatenate([low, block, high], axis=dim)  4.03 us
  transfers between devices with their start and end apart: 12, of which 7 were waited for; matrix products, arithmetic and copies ran while one was open for 37% of the time, Pallas kernels for 0%

profile of v1, /device:TPU:1, one launch (start us, length us, event | category | flops | bytes accessed | tf_op | source)
XLA Modules:
  0.0 151.8 jit_solution(15144571852403698903)
XLA Ops:
  6.5 2.1 %collective-permute-start.2 = (bf16[3,3,256,32]{2,3,1,0:T(8,128)(2,1)}, bf16[3,3,256,32]{2,3,1,0:T(8,128)(2,1)S(1)}, u32[]{:S(2)}, u32[]{:S(2)}) collective-permute-start(bf16[3,3,256,32]{2,3,1,0:T(8,128)(2,1)} %param.6), channel_id=1, source_target_pairs={{0,4},{4,8},{8,12},{12,16},{16,20},{20,24},{24,28},{28,0},{1,5},{5... | collective-permute-start | bytes 442376 | tf_op jit(solution)/shard_map/ppermute | solution.py:57
  8.6 6.9 %collective-permute-done.2 = bf16[3,3,256,32]{2,3,1,0:T(8,128)(2,1)S(1)} collective-permute-done((bf16[3,3,256,32]{2,3,1,0:T(8,128)(2,1)}, bf16[3,3,256,32]{2,3,1,0:T(8,128)(2,1)S(1)}, u32[]{:S(2)}, u32[]{:S(2)}) %collective-permute-start.2) | collective-permute-done | bytes 147488 | tf_op jit(solution)/shard_map/ppermute | solution.py:57
  15.5 4.2 %collective-permute-start.6 = (bf16[3,3,256,32]{2,3,1,0:T(8,128)(2,1)}, bf16[3,3,256,32]{2,3,1,0:T(8,128)(2,1)S(1)}, u32[]{:S(2)}, u32[]{:S(2)}) collective-permute-start(bf16[3,3,256,32]{2,3,1,0:T(8,128)(2,1)} %param.6), channel_id=1, source_target_pairs={{4,0},{8,4},{12,8},{16,12},{20,16},{24,20},{28,24},{0,28},{5,1},{9... | collective-permute-start | bytes 442376 | tf_op jit(solution)/shard_map/ppermute | solution.py:59
  19.7 2.6 %collective-permute-done.3 = bf16[3,3,256,32]{2,3,1,0:T(8,128)(2,1)S(1)} collective-permute-done((bf16[3,3,256,32]{2,3,1,0:T(8,128)(2,1)S(1)}, bf16[3,3,256,32]{2,3,1,0:T(8,128)(2,1)S(1)}, u32[]{:S(2)}, u32[]{:S(2)}) %collective-permute-start.3) | collective-permute-done | bytes 147488 | tf_op jit(solution)/shard_map/ppermute | solution.py:57
  22.3 3.0 %fusion.52 = (bf16[1,8,256,256]{3,2,1,0:T(8,128)(2,1)}, bf16[1,8,256,256]{3,2,1,0:T(8,128)(2,1)}) fusion(bf16[1,16,256,256]{3,2,1,0:T(8,128)(2,1)} %param.5), kind=kLoop, calls=%fused_computation.102 | loop fusion | bytes 4194304 | tf_op jit(solution)/shard_map/slice | solution.py:21
  25.3 5.8 %collective-permute-start = (bf16[1,8,256,256]{3,2,1,0:T(8,128)(2,1)}, bf16[1,8,256,256]{3,2,1,0:T(8,128)(2,1)}, u32[]{:S(2)}, u32[]{:S(2)}) collective-permute-start(bf16[1,8,256,256]{3,2,1,0:T(8,128)(2,1)} %get-tuple-element.7), channel_id=1, source_target_pairs={{0,1},{1,2},{2,3},{4,5},{5,6},{6,7},{8,9},{9,10},{10,11},{12,13},{... | collective-permute-start | bytes 3145736 | tf_op jit(solution)/shard_map/ppermute | solution.py:20
  33.1 4.0 %collective-permute-start.7 = (bf16[3,3,256,32]{2,3,1,0:T(8,128)(2,1)S(1)}, bf16[3,3,256,32]{2,3,1,0:T(8,128)(2,1)S(1)}, u32[]{:S(2)}, u32[]{:S(2)}) collective-permute-start(bf16[3,3,256,32]{2,3,1,0:T(8,128)(2,1)S(1)} %collective-permute-done.6), channel_id=1, source_target_pairs={{4,0},{8,4},{12,8},{16,12},{20,16},{24,20},{28,24},{0,28},{5,1},{9... | collective-permute-start | bytes 442376 | tf_op jit(solution)/shard_map/ppermute | solution.py:59
  37.2 2.8 %collective-permute-done.7 = bf16[3,3,256,32]{2,3,1,0:T(8,128)(2,1)S(1)} collective-permute-done((bf16[3,3,256,32]{2,3,1,0:T(8,128)(2,1)S(1)}, bf16[3,3,256,32]{2,3,1,0:T(8,128)(2,1)S(1)}, u32[]{:S(2)}, u32[]{:S(2)}) %collective-permute-start.7) | collective-permute-done | bytes 147488 | tf_op jit(solution)/shard_map/ppermute | solution.py:59
  39.9 4.7 %collective-permute-start.8 = (bf16[3,3,256,32]{2,3,1,0:T(8,128)(2,1)S(1)}, bf16[3,3,256,32]{2,3,1,0:T(8,128)(2,1)S(1)}, u32[]{:S(2)}, u32[]{:S(2)}) collective-permute-start(bf16[3,3,256,32]{2,3,1,0:T(8,128)(2,1)S(1)} %collective-permute-done.7), channel_id=1, source_target_pairs={{4,0},{8,4},{12,8},{16,12},{20,16},{24,20},{28,24},{0,28},{5,1},{9... | collective-permute-start | bytes 442376 | tf_op jit(solution)/shard_map/ppermute | solution.py:59
  50.5 2.0 %gather_fusion = bf16[8,3,3,256,32]{3,4,2,1,0:T(8,128)(2,1)S(1)} fusion(bf16[8,3,3,256,32]{3,4,2,1,0:T(8,128)(2,1)} %bitcast_dynamic-update-slice_fusion, s32[1024]{0:T(1024)S(1)} %pad_clamp_fusion), kind=kCustom, calls=%fused_computation | custom fusion | bytes 2359328 | tf_op jit(solution)/shard_map/gather | solution.py:62
  52.7 2.7 %fusion.41 = f32[256,16,256]{0,2,1:T(8,128)} fusion(bf16[1,16,256,256]{3,2,1,0:T(8,128)(2,1)S(1)} %copy-done, bf16[3,3,256,256]{2,3,1,0:T(8,128)(2,1)S(1)} %bitcast.210), kind=kOutput, calls=%fused_computation.60 | convolution fusion | flops 536870912 | bytes 6422528 | tf_op jit(solution)/shard_map/shwc,co->shwo/dot_general | solution.py:40
  55.4 2.1 %fusion.5 = bf16[1,32,272,256]{3,2,1,0:T(8,128)(2,1)S(1)} fusion(bf16[1,8,256,256]{3,2,1,0:T(8,128)(2,1)} %collective-permute-done.1, bf16[1,16,256,256]{3,2,1,0:T(8,128)(2,1)S(1)} %copy-done, bf16[1,8,256,256]{3,2,1,0:T(8,128)(2,1)} %collective-permute-done), kind=kLoop, calls=%fused_computation.10 | loop fusion | flops 26738688 | bytes 8650752 | tf_op jit(solution)/shard_map/concatenate | solution.py:24
  57.5 2.7 %fusion.32 = f32[16,256,256]{2,1,0:T(8,128)} fusion(bf16[1,32,272,256]{3,2,1,0:T(8,128)(2,1)S(1)} %fusion.5, bf16[3,3,256,256]{2,3,1,0:T(8,128)(2,1)S(1)} %bitcast.211), kind=kOutput, calls=%fused_computation.47 | convolution fusion | flops 536870912 | bytes 6422528 | tf_op jit(solution)/shard_map/shwc,co->shwo/dot_general | solution.py:40
  60.2 2.7 %fusion.33 = f32[16,256,256]{2,1,0:T(8,128)} fusion(bf16[1,32,272,256]{3,2,1,0:T(8,128)(2,1)S(1)} %fusion.5, bf16[3,3,256,256]{2,3,1,0:T(8,128)(2,1)S(1)} %bitcast.212), kind=kOutput, calls=%fused_computation.49 | convolution fusion | flops 536870912 | bytes 6422528 | tf_op jit(solution)/shard_map/shwc,co->shwo/dot_general | solution.py:40
  62.9 2.7 %fusion.34 = f32[16,256,256]{2,1,0:T(8,128)} fusion(bf16[1,32,272,256]{3,2,1,0:T(8,128)(2,1)S(1)} %fusion.5, bf16[3,3,256,256]{2,3,1,0:T(8,128)(2,1)S(1)} %bitcast.213), kind=kOutput, calls=%fused_computation.51 | convolution fusion | flops 536870912 | bytes 6422528 | tf_op jit(solution)/shard_map/shwc,co->shwo/dot_general | solution.py:40
  65.6 2.7 %fusion.35 = f32[16,256,256]{2,1,0:T(8,128)} fusion(bf16[1,32,272,256]{3,2,1,0:T(8,128)(2,1)S(1)} %fusion.5, bf16[3,3,256,256]{2,3,1,0:T(8,128)(2,1)S(1)} %bitcast.214), kind=kOutput, calls=%fused_computation.53 | convolution fusion | flops 536870912 | bytes 6422528 | tf_op jit(solution)/shard_map/shwc,co->shwo/dot_general | solution.py:40
  68.3 2.7 %fusion.40 = f32[16,256,256]{2,1,0:T(8,128)} fusion(bf16[1,32,272,256]{3,2,1,0:T(8,128)(2,1)S(1)} %fusion.5, bf16[3,3,256,256]{2,3,1,0:T(8,128)(2,1)S(1)} %bitcast.215), kind=kOutput, calls=%fused_computation.59 | convolution fusion | flops 536870912 | bytes 6422528 | tf_op jit(solution)/shard_map/shwc,co->shwo/dot_general | solution.py:40
  71.0 3.9 %fusion.37 = f32[16,256,256]{2,1,0:T(8,128)} fusion(bf16[1,16,256,256]{3,2,1,0:T(8,128)(2,1)S(1)} %copy-done, bf16[1,8,256,256]{3,2,1,0:T(8,128)(2,1)} %collective-permute-done, bf16[3,3,256,256]{2,3,1,0:T(8,128)(2,1)S(1)} %bitcast.216), kind=kOutput, calls=%fused_computation.56 | convolution fusion | flops 537919488 | bytes 7471104 | tf_op jit(solution)/shard_map/shwc,co->shwo/dot_general | solution.py:40
  74.9 3.9 %fusion.29 = f32[16,256,256]{2,1,0:T(8,128)} fusion(bf16[1,8,256,256]{3,2,1,0:T(8,128)(2,1)} %collective-permute-done.1, bf16[1,16,256,256]{3,2,1,0:T(8,128)(2,1)S(1)} %copy-done, bf16[3,3,256,256]{2,3,1,0:T(8,128)(2,1)S(1)} %bitcast.217), kind=kOutput, calls=%fused_computation.44 | convolution fusion | flops 537919488 | bytes 7471104 | tf_op jit(solution)/shard_map/shwc,co->shwo/dot_general | solution.py:40
  78.9 11.8 %fusion.12 = bf16[16,256,256]{2,1,0:T(8,128)(2,1)S(1)} fusion(f32[16,256,256]{2,1,0:T(8,128)} %fusion.29, f32[16,256,256]{2,1,0:T(8,128)} %fusion.32, f32[16,256,256]{2,1,0:T(8,128)} %fusion.33, f32[256,16,256]{0,2,1:T(8,128)} %fusion.41, f32[16,256,256]{2,1,0:T(8,128)} %fusion.34, f32[16,256,256]{2,1,0:T(8,128)} %fusion.35, f32[16,256,256]{2,1,0:T(8,128)} %fusion.40, ...), kind=kOutput, calls=%fused_computation.18 | convolution fusion | flops 548405248 | bytes 37880832 | tf_op jit(solution)/shard_map/shwc,co->shwo/dot_general | solution.py:40
  92.1 4.2 %collective-permute-start.9 = (bf16[1,8,256,256]{3,2,1,0:T(8,128)(2,1)}, bf16[1,8,256,256]{3,2,1,0:T(8,128)(2,1)S(1)}, u32[]{:S(2)}, u32[]{:S(2)}) collective-permute-start(bf16[1,8,256,256]{3,2,1,0:T(8,128)(2,1)} %get-tuple-element.5), channel_id=1, source_target_pairs={{0,1},{1,2},{2,3},{4,5},{5,6},{6,7},{8,9},{9,10},{10,11},{12,13},{... | collective-permute-start | bytes 3145736 | tf_op jit(solution)/shard_map/ppermute | solution.py:20
  96.3 2.1 %collective-permute-start.10 = (bf16[1,8,256,256]{3,2,1,0:T(8,128)(2,1)}, bf16[1,8,256,256]{3,2,1,0:T(8,128)(2,1)}, u32[]{:S(2)}, u32[]{:S(2)}) collective-permute-start(bf16[1,8,256,256]{3,2,1,0:T(8,128)(2,1)} %get-tuple-element.6), channel_id=1, source_target_pairs={{1,0},{2,1},{3,2},{5,4},{6,5},{7,6},{9,8},{10,9},{11,10},{13,12},{... | collective-permute-start | bytes 3145736 | tf_op jit(solution)/shard_map/ppermute | solution.py:23
  98.4 3.7 %fusion.44 = f32[16,256,256]{2,1,0:T(8,128)} fusion(bf16[16,256,256]{2,1,0:T(8,128)(2,1)S(1)} %fusion.12, bf16[3,3,256,256]{2,3,1,0:T(8,128)(2,1)} %all-gather.2.cloned.1.call-done), kind=kOutput, calls=%fused_computation.76 | convolution fusion | flops 536870912 | bytes 6422528 | tf_op jit(solution)/shard_map/shwc,co->shwo/dot_general | solution.py:40
  102.1 6.2 %collective-permute-done.9 = bf16[1,8,256,256]{3,2,1,0:T(8,128)(2,1)S(1)} collective-permute-done((bf16[1,8,256,256]{3,2,1,0:T(8,128)(2,1)}, bf16[1,8,256,256]{3,2,1,0:T(8,128)(2,1)S(1)}, u32[]{:S(2)}, u32[]{:S(2)}) %collective-permute-start.9) | collective-permute-done | bytes 1048608 | tf_op jit(solution)/shard_map/ppermute | solution.py:20
  108.3 2.7 %fusion.23 = f32[16,256,256]{2,1,0:T(8,128)} fusion(bf16[1,16,256,256]{3,2,1,0:T(8,128)(2,1)S(1)} %bitcast.206, bf16[1,8,256,256]{3,2,1,0:T(8,128)(2,1)S(1)} %collective-permute-done.9, bf16[3,3,256,256]{2,3,1,0:T(8,128)(2,1)S(1)} %copy-done.2), kind=kOutput, calls=%fused_computation.36 | convolution fusion | flops 537919488 | bytes 7471104 | tf_op jit(solution)/shard_map/shwc,co->shwo/dot_general | solution.py:40
  112.7 4.0 %fusion.15 = f32[16,256,256]{2,1,0:T(8,128)} fusion(bf16[1,8,256,256]{3,2,1,0:T(8,128)(2,1)} %collective-permute-done.10, bf16[1,16,256,256]{3,2,1,0:T(8,128)(2,1)S(1)} %bitcast.207, bf16[3,3,256,256]{2,3,1,0:T(8,128)(2,1)S(1)} %copy-done.2), kind=kOutput, calls=%fused_computation.24 | convolution fusion | flops 537919488 | bytes 7471104 | tf_op jit(solution)/shard_map/shwc,co->shwo/dot_general | solution.py:40
  118.6 2.7 %fusion.18 = f32[16,256,256]{2,1,0:T(8,128)} fusion(bf16[1,32,272,256]{3,2,1,0:T(8,128)(2,1)S(1)} %select_maximum_fusion, bf16[3,3,256,256]{2,3,1,0:T(8,128)(2,1)S(1)} %copy-done.2), kind=kOutput, calls=%fused_computation.27 | convolution fusion | flops 536870912 | bytes 6422528 | tf_op jit(solution)/shard_map/shwc,co->shwo/dot_general | solution.py:40
  121.3 2.7 %fusion.19 = f32[16,256,256]{2,1,0:T(8,128)} fusion(bf16[1,32,272,256]{3,2,1,0:T(8,128)(2,1)S(1)} %select_maximum_fusion, bf16[3,3,256,256]{2,3,1,0:T(8,128)(2,1)S(1)} %copy-done.2), kind=kOutput, calls=%fused_computation.29 | convolution fusion | flops 536870912 | bytes 6422528 | tf_op jit(solution)/shard_map/shwc,co->shwo/dot_general | solution.py:40
  124.0 2.7 %fusion.20 = f32[16,256,256]{2,1,0:T(8,128)} fusion(bf16[1,32,272,256]{3,2,1,0:T(8,128)(2,1)S(1)} %select_maximum_fusion, bf16[3,3,256,256]{2,3,1,0:T(8,128)(2,1)S(1)} %copy-done.2), kind=kOutput, calls=%fused_computation.31 | convolution fusion | flops 536870912 | bytes 6422528 | tf_op jit(solution)/shard_map/shwc,co->shwo/dot_general | solution.py:40
  126.7 2.7 %fusion.21 = f32[16,256,256]{2,1,0:T(8,128)} fusion(bf16[1,32,272,256]{3,2,1,0:T(8,128)(2,1)S(1)} %select_maximum_fusion, bf16[3,3,256,256]{2,3,1,0:T(8,128)(2,1)S(1)} %copy-done.2), kind=kOutput, calls=%fused_computation.33 | convolution fusion | flops 536870912 | bytes 6422528 | tf_op jit(solution)/shard_map/shwc,co->shwo/dot_general | solution.py:40
  129.4 2.8 %fusion.26 = f32[16,256,256]{2,1,0:T(8,128)} fusion(bf16[1,32,272,256]{3,2,1,0:T(8,128)(2,1)S(1)} %select_maximum_fusion, bf16[3,3,256,256]{2,3,1,0:T(8,128)(2,1)S(1)} %copy-done.2), kind=kOutput, calls=%fused_computation.39 | convolution fusion | flops 536870912 | bytes 6422528 | tf_op jit(solution)/shard_map/shwc,co->shwo/dot_general | solution.py:40
  132.8 12.1 %fusion.43 = bf16[1,16,256,256]{3,2,1,0:T(8,128)(2,1)} fusion(f32[256]{0:T(256)S(1)} %copy-done.5, bf16[1,32,272,256]{3,2,1,0:T(8,128)(2,1)S(1)} %select_maximum_fusion, f32[16,256,256]{2,1,0:T(8,128)} %fusion.15, f32[16,256,256]{2,1,0:T(8,128)} %fusion.18, f32[16,256,256]{2,1,0:T(8,128)} %fusion.19, f32[16,256,256]{2,1,0:T(8,128)} %fusion.44, ...), kind=kOutput, calls=%fused_computation.62 | convolution fusion | flops 548405248 | bytes 37880832 | tf_op jit(solution)/shard_map/shwc,co->shwo/dot_general | solution.py:40
  (39 shorter events, 13.7 us)
Async XLA Ops:
  6.5 41.1 %copy-start.3 = (bf16[3,3,256,32]{2,3,1,0:T(8,128)(2,1)S(1)}, bf16[3,3,256,32]{2,3,1,0:T(8,128)(2,1)}, u32[]{:S(2)}) copy-start(bf16[3,3,256,32]{2,3,1,0:T(8,128)(2,1)} %param.6) | copy-start | bytes 442372
  6.5 91.9 %all-gather.2.cloned.1.call-start = ((), (), s32[]{:S(2)}) async-start(), calls=%async_computation | async-start | bytes 1327104 | tf_op jit(solution)/shard_map/all_gather | solution.py:68
  6.5 9.0 %collective-permute-start.2 = (bf16[3,3,256,32]{2,3,1,0:T(8,128)(2,1)}, bf16[3,3,256,32]{2,3,1,0:T(8,128)(2,1)S(1)}, u32[]{:S(2)}, u32[]{:S(2)}) collective-permute-start(bf16[3,3,256,32]{2,3,1,0:T(8,128)(2,1)} %param.6), channel_id=1, source_target_pairs={{0,4},{4,8},{8,12},{12,16},{16,20},{20,24},{24,28},{28,0},{1,5},{5... | collective-permute-start | bytes 442376 | tf_op jit(solution)/shard_map/ppermute | solution.py:57
  15.5 6.8 %collective-permute-start.3 = (bf16[3,3,256,32]{2,3,1,0:T(8,128)(2,1)S(1)}, bf16[3,3,256,32]{2,3,1,0:T(8,128)(2,1)S(1)}, u32[]{:S(2)}, u32[]{:S(2)}) collective-permute-start(bf16[3,3,256,32]{2,3,1,0:T(8,128)(2,1)S(1)} %collective-permute-done.2), channel_id=1, source_target_pairs={{0,4},{4,8},{8,12},{12,16},{16,20},{20,24},{24,28},{28,0},{1,5},{5... | collective-permute-start | bytes 442376 | tf_op jit(solution)/shard_map/ppermute | solution.py:57
  15.5 17.6 %collective-permute-start.6 = (bf16[3,3,256,32]{2,3,1,0:T(8,128)(2,1)}, bf16[3,3,256,32]{2,3,1,0:T(8,128)(2,1)S(1)}, u32[]{:S(2)}, u32[]{:S(2)}) collective-permute-start(bf16[3,3,256,32]{2,3,1,0:T(8,128)(2,1)} %param.6), channel_id=1, source_target_pairs={{4,0},{8,4},{12,8},{16,12},{20,16},{24,20},{28,24},{0,28},{5,1},{9... | collective-permute-start | bytes 442376 | tf_op jit(solution)/shard_map/ppermute | solution.py:59
  22.3 14.8 %collective-permute-start.4 = (bf16[3,3,256,32]{2,3,1,0:T(8,128)(2,1)S(1)}, bf16[3,3,256,32]{2,3,1,0:T(8,128)(2,1)S(1)}, u32[]{:S(2)}, u32[]{:S(2)}) collective-permute-start(bf16[3,3,256,32]{2,3,1,0:T(8,128)(2,1)S(1)} %collective-permute-done.3), channel_id=1, source_target_pairs={{0,4},{4,8},{8,12},{12,16},{16,20},{20,24},{24,28},{28,0},{1,5},{5... | collective-permute-start | bytes 442376 | tf_op jit(solution)/shard_map/ppermute | solution.py:57
  25.3 30.0 %collective-permute-start = (bf16[1,8,256,256]{3,2,1,0:T(8,128)(2,1)}, bf16[1,8,256,256]{3,2,1,0:T(8,128)(2,1)}, u32[]{:S(2)}, u32[]{:S(2)}) collective-permute-start(bf16[1,8,256,256]{3,2,1,0:T(8,128)(2,1)} %get-tuple-element.7), channel_id=1, source_target_pairs={{0,1},{1,2},{2,3},{4,5},{5,6},{6,7},{8,9},{9,10},{10,11},{12,13},{... | collective-permute-start | bytes 3145736 | tf_op jit(solution)/shard_map/ppermute | solution.py:20
  31.1 24.2 %collective-permute-start.1 = (bf16[1,8,256,256]{3,2,1,0:T(8,128)(2,1)}, bf16[1,8,256,256]{3,2,1,0:T(8,128)(2,1)}, u32[]{:S(2)}, u32[]{:S(2)}) collective-permute-start(bf16[1,8,256,256]{3,2,1,0:T(8,128)(2,1)} %get-tuple-element.8), channel_id=1, source_target_pairs={{1,0},{2,1},{3,2},{5,4},{6,5},{7,6},{9,8},{10,9},{11,10},{13,12},{... | collective-permute-start | bytes 3145736 | tf_op jit(solution)/shard_map/ppermute | solution.py:23
  33.1 6.8 %collective-permute-start.7 = (bf16[3,3,256,32]{2,3,1,0:T(8,128)(2,1)S(1)}, bf16[3,3,256,32]{2,3,1,0:T(8,128)(2,1)S(1)}, u32[]{:S(2)}, u32[]{:S(2)}) collective-permute-start(bf16[3,3,256,32]{2,3,1,0:T(8,128)(2,1)S(1)} %collective-permute-done.6), channel_id=1, source_target_pairs={{4,0},{8,4},{12,8},{16,12},{20,16},{24,20},{28,24},{0,28},{5,1},{9... | collective-permute-start | bytes 442376 | tf_op jit(solution)/shard_map/ppermute | solution.py:59
  37.1 7.8 %collective-permute-start.5 = (bf16[3,3,256,32]{2,3,1,0:T(8,128)(2,1)S(1)}, bf16[3,3,256,32]{2,3,1,0:T(8,128)(2,1)S(1)}, u32[]{:S(2)}, u32[]{:S(2)}) collective-permute-start(bf16[3,3,256,32]{2,3,1,0:T(8,128)(2,1)S(1)} %collective-permute-done.4), channel_id=1, source_target_pairs={{0,4},{4,8},{8,12},{12,16},{16,20},{20,24},{24,28},{28,0},{1,5},{5... | collective-permute-start | bytes 442376 | tf_op jit(solution)/shard_map/ppermute | solution.py:57
  39.9 9.9 %collective-permute-start.8 = (bf16[3,3,256,32]{2,3,1,0:T(8,128)(2,1)S(1)}, bf16[3,3,256,32]{2,3,1,0:T(8,128)(2,1)S(1)}, u32[]{:S(2)}, u32[]{:S(2)}) collective-permute-start(bf16[3,3,256,32]{2,3,1,0:T(8,128)(2,1)S(1)} %collective-permute-done.7), channel_id=1, source_target_pairs={{4,0},{8,4},{12,8},{16,12},{20,16},{24,20},{28,24},{0,28},{5,1},{9... | collective-permute-start | bytes 442376 | tf_op jit(solution)/shard_map/ppermute | solution.py:59
  50.5 2.2 %copy-start = (bf16[1,16,256,256]{3,2,1,0:T(8,128)(2,1)S(1)}, bf16[1,16,256,256]{3,2,1,0:T(8,128)(2,1)}, u32[]{:S(2)}) copy-start(bf16[1,16,256,256]{3,2,1,0:T(8,128)(2,1)} %param.5) | copy-start | bytes 6291460
  74.9 3.9 %copy-start.4 = (f32[256]{0:T(256)S(1)}, f32[256]{0:T(256)}, u32[]{:S(2)}) copy-start(f32[256]{0:T(256)} %param.7) | copy-start | bytes 3076
  92.1 16.2 %collective-permute-start.9 = (bf16[1,8,256,256]{3,2,1,0:T(8,128)(2,1)}, bf16[1,8,256,256]{3,2,1,0:T(8,128)(2,1)S(1)}, u32[]{:S(2)}, u32[]{:S(2)}) collective-permute-start(bf16[1,8,256,256]{3,2,1,0:T(8,128)(2,1)} %get-tuple-element.5), channel_id=1, source_target_pairs={{0,1},{1,2},{2,3},{4,5},{5,6},{6,7},{8,9},{9,10},{10,11},{12,13},{... | collective-permute-start | bytes 3145736 | tf_op jit(solution)/shard_map/ppermute | solution.py:20
  96.3 16.4 %collective-permute-start.10 = (bf16[1,8,256,256]{3,2,1,0:T(8,128)(2,1)}, bf16[1,8,256,256]{3,2,1,0:T(8,128)(2,1)}, u32[]{:S(2)}, u32[]{:S(2)}) collective-permute-start(bf16[1,8,256,256]{3,2,1,0:T(8,128)(2,1)} %get-tuple-element.6), channel_id=1, source_target_pairs={{1,0},{2,1},{3,2},{5,4},{6,5},{7,6},{9,8},{10,9},{11,10},{13,12},{... | collective-permute-start | bytes 3145736 | tf_op jit(solution)/shard_map/ppermute | solution.py:23
  98.4 9.9 %copy-start.2 = (bf16[3,3,256,256]{2,3,1,0:T(8,128)(2,1)S(1)}, bf16[3,3,256,256]{2,3,1,0:T(8,128)(2,1)}, u32[]{:S(2)}) copy-start(bf16[3,3,256,256]{2,3,1,0:T(8,128)(2,1)} %all-gather.2.cloned.1.call-done) | copy-start | bytes 3538948
  129.4 3.4 %copy-start.1 = (f32[16,256,256]{2,1,0:T(8,128)S(1)}, f32[16,256,256]{2,1,0:T(8,128)}, u32[]{:S(2)}) copy-start(f32[16,256,256]{2,1,0:T(8,128)} %fusion.23) | copy-start | bytes 12582916
  129.4 3.4 %copy-start.5 = (f32[256]{0:T(256)S(1)}, f32[256]{0:T(256)}, u32[]{:S(2)}) copy-start(f32[256]{0:T(256)} %param.9) | copy-start | bytes 3076
Sparse Core Ops, SparseCore 0:
  33.2 42.0 all-gather.1
